TPU v7x, 32 devices: a whole 2x2x4 slice. The times are simulated.
32 devices in a mesh: seg: 4 (over z), blk: 8 (over y, x, core).
Axes of the slice: x: 2, y: 2, z: 4, core: 2. Of those that a mesh axis runs over, the one named last changes fastest.
Arguments:
- train_acts: bfloat16 [4, 1024, 512], P('seg', 'blk'), may hold values from -6 to 6
- train_grads: bfloat16 [4, 1024, 4096], P('seg', 'blk'), may hold values from -0.0059814453 to 0.0059814453
- counts: int32 [8], replicated, may hold values from 1 to 2, as said below
- basis_in: bfloat16 [4, 1, 512, 512], P('seg'), may hold values from -1 to 1, as said below
- basis_out: bfloat16 [4, 8, 512, 512], P('seg', 'blk'), may hold values from -1 to 1, as said below
- eigenvalues: bfloat16 [4, 8, 512, 512], P('seg', 'blk'), may hold values from 0.049804688 to 5
- back_weight: bfloat16 [4, 8, 512, 512], P('seg', 'blk'), may hold values from -0.25 to 0.25
- derivative: bfloat16 [4, 4, 32, 4096], P('seg', None, None, 'blk'), may hold values from 0 to 1
- query_acts: bfloat16 [4, 4, 32, 512], P('seg'), may hold values from -6 to 6
- query_top: bfloat16 [4, 32, 4096], P(None, None, 'blk'), may hold values from -0.0059814453 to 0.0059814453
Outputs:
- scores: float32 [4, 16], P(None, 'blk')
Inputs may be any that keep to these rules, and one draw needn't show every extreme that they name: In each pair of indices 2k and 2k+1 of blk one count is 2 and the other 1, so all counts add up to 12; slots below a device's count are valid. `basis_in`: each 512 x 512 matrix is orthogonal up to rounding. `basis_out`: each 512 x 512 matrix is orthogonal up to rounding.
All inputs are finite; a program needn't handle non-finite values.
Results may differ from a plain program's by a relative error of at most 0.015.
Values may be sent and summed in bfloat16 or wider, within the bound.
A program may use at most 64 MiB of HBM per device.

v0:
```python
import math
import jax
import jax.numpy as jnp
from jax import lax
from jax.sharding import PartitionSpec as P

TB = 64
SLOTS = 2
damping = 0.05


def passed_along(value, axis, steps):
    count = lax.axis_size(axis)
    first, last = (max(0, -steps), min(count, count - steps))
    return lax.ppermute(value, axis, [(source, source + steps) for source in range(first, last)])


def advance(current, weight, derivs):
    queries, query_tok, blk_width = current.shape
    mixed = jnp.dot(
        current.reshape(queries * query_tok, blk_width), weight, preferred_element_type=jnp.float32
    )
    mixed = mixed.reshape(queries, query_tok, blk_width)
    return (current.astype(jnp.float32) + mixed * derivs.astype(jnp.float32)).astype(jnp.bfloat16)


def precondition(current, acts_seg, inner_basis, outer_basis, eigen_block):
    queries, query_tok, blk_width = current.shape
    in_slices = inner_basis.shape[0]
    in_width = in_slices * blk_width
    rot_err = jnp.dot(
        current.reshape(queries * query_tok, blk_width),
        outer_basis,
        preferred_element_type=jnp.float32,
    )
    rot_err = rot_err.astype(jnp.bfloat16).reshape(queries, query_tok, blk_width)
    act_split = acts_seg.reshape(queries, query_tok, in_slices, blk_width)
    rot_acts = jnp.einsum(
        "qtid,ide->qtie", act_split, inner_basis, preferred_element_type=jnp.float32
    ).astype(jnp.bfloat16)
    core_raw = jnp.einsum("qtd,qtie->qdie", rot_err, rot_acts, preferred_element_type=jnp.float32)
    core_raw = core_raw.reshape(queries, blk_width, in_width)
    scaled_core = (core_raw / (eigen_block.astype(jnp.float32)[None] + damping)).astype(
        jnp.bfloat16
    )
    left_prod = jnp.einsum(
        "cd,qdf->qcf", outer_basis, scaled_core, preferred_element_type=jnp.float32
    ).astype(jnp.bfloat16)
    left_split = left_prod.reshape(queries, blk_width, in_slices, blk_width)
    precond = jnp.einsum(
        "qcie,ife->qcif", left_split, inner_basis, preferred_element_type=jnp.float32
    )
    return precond.astype(jnp.bfloat16).reshape(queries, blk_width, in_width)


def block_scores(grad_rows, act_rows, precond, slot_tokens):
    row_count = grad_rows.shape[0]
    group_count = max(row_count // slot_tokens, 1)
    group_rows = row_count // group_count
    batch_groups = math.gcd(group_count, 8)
    grad_groups = grad_rows.reshape(
        group_count // batch_groups, batch_groups, group_rows, grad_rows.shape[1]
    )
    act_groups = act_rows.reshape(
        group_count // batch_groups, batch_groups, group_rows, act_rows.shape[1]
    )

    def one_batch(operands):
        grad_block, act_block = operands
        outer_prod = jnp.einsum(
            "btd,bte->bde", grad_block, act_block, preferred_element_type=jnp.float32
        ).astype(jnp.bfloat16)
        return jnp.einsum("bde,qde->bq", outer_prod, precond, preferred_element_type=jnp.float32)

    partial_scores = lax.map(one_batch, (grad_groups, act_groups))
    return (partial_scores.reshape(group_count, precond.shape[0]), group_rows)


def body(
    train_acts,
    train_grads,
    counts,
    basis_in,
    basis_out,
    eigenvalues,
    back_weight,
    derivative,
    query_acts,
    query_top,
):
    seg_count = lax.axis_size("seg")
    seg_index = lax.axis_index("seg")
    blk_index = lax.axis_index("blk")
    n_slot = lax.axis_size("blk") * SLOTS
    slot_ids = jnp.arange(n_slot, dtype=jnp.int32)
    current = query_top
    for relay_step in range(seg_count - 1):
        moved = advance(current, back_weight[0, 0], derivative[0])
        arrived = passed_along(moved, "seg", -1)
        current = jnp.where(seg_index == seg_count - 2 - relay_step, arrived, current)
    precond = precondition(current, query_acts[0], basis_in[0], basis_out[0, 0], eigenvalues[0, 0])
    exchanged = lax.all_to_all(train_grads, "blk", split_axis=2, concat_axis=1, tiled=True)
    grad_rows = exchanged[0]
    scores_part, group_rows = block_scores(
        grad_rows, lax.all_gather(train_acts, "blk", axis=1, tiled=True)[0], precond, TB
    )
    slot_of = jnp.arange(scores_part.shape[0], dtype=jnp.int32) * group_rows // TB
    placement = (slot_of[:, None] == slot_ids[None, :]).astype(jnp.float32)
    local_scores = jnp.dot(scores_part.T, placement, precision=lax.Precision.HIGHEST)
    mine = lax.psum_scatter(local_scores, "blk", scatter_dimension=1, tiled=True)
    mine = lax.psum(mine, "seg")
    own_valid = (jnp.arange(SLOTS, dtype=jnp.int32) < counts[blk_index]).astype(jnp.float32)
    return mine * own_valid[None, :]


def solution(mesh):
    in_specs = (
        P("seg", "blk", None),
        P("seg", "blk", None),
        P(),
        P("seg", None, None, None),
        P("seg", "blk", None, None),
        P("seg", "blk", None, None),
        P("seg", "blk", None, None),
        P("seg", None, None, "blk"),
        P("seg", None, None, None),
        P(None, None, "blk"),
    )
    out_specs = P(None, "blk")
    return jax.shard_map(body, mesh=mesh, in_specs=in_specs, out_specs=out_specs, check_vma=False)
```

profile of v0, /device:TPU:0, one launch (start us, length us, event | category | flops | bytes accessed | tf_op | source)
XLA Modules:
  0.0 125.0 jit_solution(6837176893961638313)
XLA Ops:
  6.5 1.4 %fusion.15 = bf16[4,32,512]{2,1,0:T(8,128)(2,1)S(1)} fusion(bf16[4,32,512]{2,1,0:T(8,128)(2,1)} %param.21, bf16[1,1,512,512]{3,2,1,0:T(8,128)(2,1)} %param.18, bf16[1,4,32,512]{3,2,1,0:T(8,128)(2,1)} %param.19), kind=kOutput, calls=%fused_computation.20 | convolution fusion | flops 67436544 | bytes 917504 | tf_op jit(solution)/shard_map/dot_general | solution.py:20
  8.0 1.3 %collective-permute-start = (bf16[4,32,512]{2,1,0:T(8,128)(2,1)S(1)}, bf16[4,32,512]{2,1,0:T(8,128)(2,1)S(1)}, u32[]{:S(2)}, u32[]{:S(2)}) collective-permute-start(bf16[4,32,512]{2,1,0:T(8,128)(2,1)S(1)} %fusion.15), channel_id=1, source_target_pairs={{8,0},{16,8},{24,16},{9,1},{17,9},{25,17},{10,2},{18,10},{26,18},{... | collective-permute-start | bytes 393224 | tf_op jit(solution)/shard_map/ppermute | solution.py:15
  9.3 5.0 %copy.25 = bf16[1,128,4096]{1,0,2:T(2,128)(2,1)S(1)} copy(bf16[1,128,4096]{2,1,0:T(8,128)(2,1)} %param.13) | data formatting | bytes 2097152 | tf_op args[1]
  14.3 0.5 broadcast.63
  14.8 23.4 %reduce = bf16[4096,128]{1,0:T(8,128)(2,1)} reduce(bf16[4096,1,128]{2,1,0:T(2,128)(2,1)S(1)} %bitcast.92, bf16[]{:T(256)} %broadcast.63), dimensions={1}, to_apply=%bitcast.73.reduce_sub_computation | reduce | bytes 2097154
  38.2 2.2 %reshape.95 = bf16[8,2,32768]{2,1,0:T(2,128)(2,1)} reshape(bf16[4096,128]{1,0:T(8,128)(2,1)} %reduce) | data formatting | bytes 2097152
  40.4 5.3 %all-to-all-start = ((bf16[8,2,32768]{2,1,0:T(2,128)(2,1)}), bf16[8,2,32768]{2,1,0:T(2,128)(2,1)}, u32[]{:S(2)}, u32[]{:S(2)}) async-start(bf16[8,2,32768]{2,1,0:T(2,128)(2,1)} %reshape.95), calls=%async_computation | async-start | bytes 2097152 | tf_op jit(solution)/shard_map/all_to_all | solution.py:102
  45.8 0.7 all-gather.2.cloned.1.call-update
  46.9 1.3 %collective-permute-start.1 = (bf16[4,32,512]{2,1,0:T(8,128)(2,1)S(1)}, bf16[4,32,512]{2,1,0:T(8,128)(2,1)S(1)}, u32[]{:S(2)}, u32[]{:S(2)}) collective-permute-start(bf16[4,32,512]{2,1,0:T(8,128)(2,1)S(1)} %add_convert_fusion.1), channel_id=1, source_target_pairs={{8,0},{16,8},{24,16},{9,1},{17,9},{25,17},{10,2},{18,10},{26,18},{... | collective-permute-start | bytes 393224 | tf_op jit(solution)/shard_map/ppermute | solution.py:15
  48.3 7.2 %collective-permute-done.1 = bf16[4,32,512]{2,1,0:T(8,128)(2,1)S(1)} collective-permute-done((bf16[4,32,512]{2,1,0:T(8,128)(2,1)S(1)}, bf16[4,32,512]{2,1,0:T(8,128)(2,1)S(1)}, u32[]{:S(2)}, u32[]{:S(2)}) %collective-permute-start.1) | collective-permute-done | bytes 131104 | tf_op jit(solution)/shard_map/ppermute | solution.py:15
  55.5 0.2 add_convert_fusion
  55.8 1.5 %collective-permute-start.2 = (bf16[4,32,512]{2,1,0:T(8,128)(2,1)S(1)}, bf16[4,32,512]{2,1,0:T(8,128)(2,1)S(1)}, u32[]{:S(2)}, u32[]{:S(2)}) collective-permute-start(bf16[4,32,512]{2,1,0:T(8,128)(2,1)S(1)} %add_convert_fusion), channel_id=1, source_target_pairs={{8,0},{16,8},{24,16},{9,1},{17,9},{25,17},{10,2},{18,10},{26,18},{... | collective-permute-start | bytes 393224 | tf_op jit(solution)/shard_map/ppermute | solution.py:15
  57.3 1.3 %fusion.16 = bf16[4,32,512]{2,1,0:T(8,128)(2,1)S(1)} fusion(bf16[1,1,512,512]{3,2,1,0:T(8,128)(2,1)} %param.15, bf16[1,4,32,512]{3,2,1,0:T(8,128)(2,1)S(1)} %copy-done.7), kind=kOutput, calls=%fused_computation.21 | convolution fusion | flops 67174400 | bytes 786432 | tf_op jit(solution)/shard_map/qtid,ide->qtie/dot_general | solution.py:38
  58.6 0.6 dynamic-slice
  59.9 0.7 dynamic_slice.10
  60.5 2.7 %collective-permute-done.2 = bf16[4,32,512]{2,1,0:T(8,128)(2,1)S(1)} collective-permute-done((bf16[4,32,512]{2,1,0:T(8,128)(2,1)S(1)}, bf16[4,32,512]{2,1,0:T(8,128)(2,1)S(1)}, u32[]{:S(2)}, u32[]{:S(2)}) %collective-permute-start.2) | collective-permute-done | bytes 131104 | tf_op jit(solution)/shard_map/ppermute | solution.py:15
  63.5 3.2 %fusion.13 = bf16[4,512,512]{2,1,0:T(8,128)(2,1)} fusion(bf16[4,32,512]{2,1,0:T(8,128)(2,1)S(1)} %bitcast.96, bf16[4,32,512]{2,1,0:T(8,128)(2,1)S(1)} %fusion.16, f32[512,512]{1,0:T(8,128)S(1)} %add_bitcast_fusion, bf16[1,1,512,512]{3,2,1,0:T(8,128)(2,1)S(1)} %copy-done), kind=kOutput, calls=%fused_computation.13 | convolution fusion | flops 1142947840 | bytes 3932160 | tf_op jit(solution)/shard_map/cd,qdf->qcf/dot_general | solution.py:46
  66.7 2.9 %fusion.10 = bf16[4,512,512]{2,1,0:T(8,128)(2,1)S(1)} fusion(bf16[4,512,512]{2,1,0:T(8,128)(2,1)} %fusion.13, bf16[1,1,512,512]{3,2,1,0:T(8,128)(2,1)S(1)} %copy-done.6), kind=kOutput, calls=%fused_computation.12 | convolution fusion | flops 1074790400 | bytes 4718592 | tf_op jit(solution)/shard_map/qcie,ife->qcif/dot_general | solution.py:50
  69.6 3.0 %copy.29 = bf16[4,512,512]{2,0,1:T(4,128)(2,1)} copy(bf16[4,512,512]{2,1,0:T(8,128)(2,1)S(1)} %fusion.10) | data formatting | bytes 4194304 | tf_op jit(solution)/shard_map/while | solution.py:75
  72.5 4.3 %reshape.96 = bf16[4096,1,128]{2,1,0:T(2,128)(2,1)S(1)} reshape(bf16[8,2,32768]{2,1,0:T(2,128)(2,1)} %all-to-all-done) | data formatting | bytes 2097152
  76.9 1.1 copy.35
  78.0 1.5 %copy.26 = bf16[1,8,128,512]{3,2,1,0:T(8,128)(2,1)S(1)} copy(bf16[1,8,128,512]{2,3,1,0:T(8,128)(2,1)} %bitcast.94) | data formatting | bytes 2097152 | tf_op jit(solution)/shard_map/all_to_all | solution.py:102
  79.5 12.8 %while.10 = (s32[]{:T(128)}, f32[2,8,4]{1,0,2:T(2,128)S(1)}, bf16[2,8,64,512]{3,2,1,0:T(8,128)(2,1)S(1)}, bf16[2,8,64,512]{3,2,1,0:T(8,128)(2,1)}, bf16[4,512,512]{2,0,1:T(4,128)(2,1)}, /*index=5*/s32[]{:T(128)}, s32[]{:T(128)}) while((s32[]{:T(128)}, f32[2,8,4]{1,0,2:T(2,128)S(1)}, bf16[2,8,64,512]{3,2,1,0:T(8,128)(2,1)S(1)}, ...), condition=%wide.region_1.2_spmd, body=%wide.region_0.1_spmd.sunk | while | flops 287309824 | bytes 19924460 | solution.py:75
  79.5 2.5 %convolution_convert_fusion.4 = bf16[8,512,512]{2,1,0:T(8,128)(2,1)S(1)} fusion(bf16[2,8,64,512]{3,2,1,0:T(8,128)(2,1)} %get-tuple-element.111, s32[]{:T(128)} %get-tuple-element.101, bf16[2,8,64,512]{3,2,1,0:T(8,128)(2,1)S(1)} %get-tuple-element.110), kind=kOutput, calls=%fused_computation.2.clone.1 | convolution fusion | flops 270532608 | bytes 5243904 | tf_op jit(solution)/shard_map/while/body/eval_jaxpr/btd,bte->bde/dot_general | solution.py:70
  82.0 3.8 %fusion.47 = f32[8,4,1]{0,1,2:T(4,128)S(1)} fusion(bf16[4,512,512]{2,0,1:T(4,128)(2,1)S(1)} %copy-done.2, bf16[8,512,512]{2,1,0:T(8,128)(2,1)S(1)} %convolution_convert_fusion.4), kind=kOutput, calls=%fused_computation.clone.1 | convolution fusion | flops 16777216 | bytes 6291584 | tf_op jit(solution)/shard_map/while/body/eval_jaxpr/bde,qde->bq/dot_general | solution.py:73
  85.9 2.5 %convolution_convert_fusion.4 = bf16[8,512,512]{2,1,0:T(8,128)(2,1)S(1)} fusion(bf16[2,8,64,512]{3,2,1,0:T(8,128)(2,1)} %get-tuple-element.111, s32[]{:T(128)} %get-tuple-element.101, bf16[2,8,64,512]{3,2,1,0:T(8,128)(2,1)S(1)} %get-tuple-element.110), kind=kOutput, calls=%fused_computation.2.clone.1 | convolution fusion | flops 270532608 | bytes 5243904 | tf_op jit(solution)/shard_map/while/body/eval_jaxpr/btd,bte->bde/dot_general | solution.py:70
  88.4 3.8 %fusion.47 = f32[8,4,1]{0,1,2:T(4,128)S(1)} fusion(bf16[4,512,512]{2,0,1:T(4,128)(2,1)S(1)} %copy-done.2, bf16[8,512,512]{2,1,0:T(8,128)(2,1)S(1)} %convolution_convert_fusion.4), kind=kOutput, calls=%fused_computation.clone.1 | convolution fusion | flops 16777216 | bytes 6291584 | tf_op jit(solution)/shard_map/while/body/eval_jaxpr/bde,qde->bq/dot_general | solution.py:73
  92.4 0.3 fusion.29
  92.6 13.1 %all-reduce = f32[4,16]{0,1:T(8,128)S(1)} all-reduce(f32[4,16]{0,1:T(8,128)S(1)} %fusion.29), channel_id=2, replica_groups=mesh['seg'=4,'blk'=8] {'blk'}, use_global_device_ids=true, to_apply=%region_2.3.clone | all-reduce | flops 64 | bytes 512
  105.7 0.7 compare_convert_fusion
  106.4 11.2 %psum.7 = f32[4,2]{0,1:T(2,128)S(1)} all-reduce(f32[4,2]{0,1:T(2,128)S(1)} %constant_dynamic-slice_fusion), channel_id=1, replica_groups=mesh['seg'=4,'blk'=8] {'seg'}, use_global_device_ids=true, to_apply=%region_3.4 | all-reduce | flops 8 | bytes 64 | tf_op jit(solution)/shard_map/psum | solution.py:111
  117.5 0.6 broadcast_multiply_fusion
  (37 shorter events, 0.9 us)
Async XLA Ops:
  6.5 56.7 %copy-start = (bf16[1,1,512,512]{3,2,1,0:T(8,128)(2,1)S(1)}, bf16[1,1,512,512]{3,2,1,0:T(8,128)(2,1)}, u32[]{:S(2)}) copy-start(bf16[1,1,512,512]{3,2,1,0:T(8,128)(2,1)} %param.16) | copy-start | bytes 1572868
  8.0 38.5 %collective-permute-start = (bf16[4,32,512]{2,1,0:T(8,128)(2,1)S(1)}, bf16[4,32,512]{2,1,0:T(8,128)(2,1)S(1)}, u32[]{:S(2)}, u32[]{:S(2)}) collective-permute-start(bf16[4,32,512]{2,1,0:T(8,128)(2,1)S(1)} %fusion.15), channel_id=1, source_target_pairs={{8,0},{16,8},{24,16},{9,1},{17,9},{25,17},{10,2},{18,10},{26,18},{... | collective-permute-start | bytes 393224 | tf_op jit(solution)/shard_map/ppermute | solution.py:15
  38.2 8.3 %copy-start.5 = (bf16[4,32,512]{2,1,0:T(8,128)(2,1)S(1)}, bf16[4,32,512]{2,1,0:T(8,128)(2,1)}, u32[]{:S(2)}) copy-start(bf16[4,32,512]{2,1,0:T(8,128)(2,1)} %param.21) | copy-start | bytes 393220
  38.2 8.4 %copy-start.1 = (bf16[1,1,512,512]{3,2,1,0:T(8,128)(2,1)S(1)}, bf16[1,1,512,512]{3,2,1,0:T(8,128)(2,1)}, u32[]{:S(2)}) copy-start(bf16[1,1,512,512]{3,2,1,0:T(8,128)(2,1)} %param.18) | copy-start | bytes 1572868
  38.2 8.4 %copy-start.4 = (bf16[1,4,32,512]{3,2,1,0:T(8,128)(2,1)S(1)}, bf16[1,4,32,512]{3,2,1,0:T(8,128)(2,1)}, u32[]{:S(2)}) copy-start(bf16[1,4,32,512]{3,2,1,0:T(8,128)(2,1)} %param.19) | copy-start | bytes 393220
  40.4 7.7 %copy-start.3 = (bf16[1,1,512,512]{3,2,1,0:T(8,128)(2,1)S(1)}, bf16[1,1,512,512]{3,2,1,0:T(8,128)(2,1)}, u32[]{:S(2)}) copy-start(bf16[1,1,512,512]{3,2,1,0:T(8,128)(2,1)} %param.17) | copy-start | bytes 1572868
  40.4 32.1 %all-to-all-start = ((bf16[8,2,32768]{2,1,0:T(2,128)(2,1)}), bf16[8,2,32768]{2,1,0:T(2,128)(2,1)}, u32[]{:S(2)}, u32[]{:S(2)}) async-start(bf16[8,2,32768]{2,1,0:T(2,128)(2,1)} %reshape.95), calls=%async_computation | async-start | bytes 2097152 | tf_op jit(solution)/shard_map/all_to_all | solution.py:102
  45.8 11.5 %copy-start.7 = (bf16[1,4,32,512]{3,2,1,0:T(8,128)(2,1)S(1)}, bf16[1,4,32,512]{3,2,1,0:T(8,128)(2,1)}, u32[]{:S(2)}) copy-start(bf16[1,4,32,512]{3,2,1,0:T(8,128)(2,1)} %param.20) | copy-start | bytes 393220
  45.8 33.7 %all-gather.2.cloned.1.call-start = ((), (), s32[]{:S(2)}) async-start(), calls=%async_computation.1 | async-start | bytes 1179648 | tf_op jit(solution)/shard_map/all_gather | solution.py:105
  46.6 12.0 %copy-start.9 = (u32[32]{0:T(128)S(1)}, u32[32]{0:T(128)}, u32[]{:S(2)}) copy-start(u32[32]{0:T(128)} %constant.56) | copy-start | bytes 388
  46.6 13.3 %copy-start.8 = (s32[8]{0:T(128)S(1)}, s32[8]{0:T(128)}, u32[]{:S(2)}) copy-start(s32[8]{0:T(128)} %param.14) | copy-start | bytes 100
  46.9 8.7 %collective-permute-start.1 = (bf16[4,32,512]{2,1,0:T(8,128)(2,1)S(1)}, bf16[4,32,512]{2,1,0:T(8,128)(2,1)S(1)}, u32[]{:S(2)}, u32[]{:S(2)}) collective-permute-start(bf16[4,32,512]{2,1,0:T(8,128)(2,1)S(1)} %add_convert_fusion.1), channel_id=1, source_target_pairs={{8,0},{16,8},{24,16},{9,1},{17,9},{25,17},{10,2},{18,10},{26,18},{... | collective-permute-start | bytes 393224 | tf_op jit(solution)/shard_map/ppermute | solution.py:15
  55.8 7.4 %collective-permute-start.2 = (bf16[4,32,512]{2,1,0:T(8,128)(2,1)S(1)}, bf16[4,32,512]{2,1,0:T(8,128)(2,1)S(1)}, u32[]{:S(2)}, u32[]{:S(2)}) collective-permute-start(bf16[4,32,512]{2,1,0:T(8,128)(2,1)S(1)} %add_convert_fusion), channel_id=1, source_target_pairs={{8,0},{16,8},{24,16},{9,1},{17,9},{25,17},{10,2},{18,10},{26,18},{... | collective-permute-start | bytes 393224 | tf_op jit(solution)/shard_map/ppermute | solution.py:15
  63.5 3.2 %copy-start.6 = (bf16[1,1,512,512]{3,2,1,0:T(8,128)(2,1)S(1)}, bf16[1,1,512,512]{3,2,1,0:T(8,128)(2,1)}, u32[]{:S(2)}) copy-start(bf16[1,1,512,512]{3,2,1,0:T(8,128)(2,1)} %param.15) | copy-start | bytes 1572868
  79.5 2.5 %copy-start.2 = (bf16[4,512,512]{2,0,1:T(4,128)(2,1)S(1)}, bf16[4,512,512]{2,0,1:T(4,128)(2,1)}, u32[]{:S(2)}) copy-start(bf16[4,512,512]{2,0,1:T(4,128)(2,1)} %get-tuple-element.112) | copy-start | bytes 6291460 | tf_op jit(solution)/shard_map/while
  85.9 2.5 %copy-start.2 = (bf16[4,512,512]{2,0,1:T(4,128)(2,1)S(1)}, bf16[4,512,512]{2,0,1:T(4,128)(2,1)}, u32[]{:S(2)}) copy-start(bf16[4,512,512]{2,0,1:T(4,128)(2,1)} %get-tuple-element.112) | copy-start | bytes 6291460 | tf_op jit(solution)/shard_map/while
Sparse Core Ops, SparseCore 0:
  48.5 26.8 all-gather.1
where the time goes:
time: 126 us; the launch traced here: 125 us
  other arithmetic  24.9 us (20%)
  blocking collectives  24.2 us (19%)
  matrix products  22.4 us (18%)
  local copies, waits for them, and re-layouts  19.1 us (15%)
  between operations  14.3 us (11%)
  waiting for transfers between devices  10.6 us (8%)
  starting transfers between devices  9.43 us (7%)
    unnamed x1, other arithmetic  23.4 us
    unnamed x25, local copies, waits for them, and re-layouts  13.9 us
    unnamed x1, blocking collectives  13.1 us
    psum x1, blocking collectives, body(): mine = lax.psum(mine, 'seg')  11.2 us
    ppermute x3, waiting for transfers between devices, passed_along(): lax.ppermute(value, axis, [(source, source + steps) for source in range(f...  9.91 us
    dot_general x2, matrix products, one_batch(): jnp.einsum('bde,qde->bq', outer_prod, precond, preferred_element_type=jnp...  7.62 us
    all_to_all x1, starting transfers between devices, body(): lax.all_to_all(train_grads, 'blk', split_axis=2, concat_axis=1, tiled=True)  5.33 us
    dot_general x2, matrix products, one_batch(): jnp.einsum('btd,bte->bde', grad_block, act_block, preferred_element_type=...  4.98 us
  transfers between devices with their start and end apart: 5, of which 2 were waited for; matrix products, arithmetic and copies ran while one was open for 40% of the time, Pallas kernels for 0%

commit v1 on v0

--- a/solution.py
+++ b/solution.py
@@ -7,6 +7,18 @@
 TB = 64
 SLOTS = 2
 damping = 0.05
+
+
+def in_blocks(x, dim, devices):
+    shape = x.shape
+    parts = x.reshape(*shape[:dim], devices, shape[dim] // devices, *shape[dim + 1 :])
+    return jnp.moveaxis(parts, dim, 0)
+
+
+def joined_along(blocks, dim):
+    shape = list(blocks.shape[1:])
+    shape[dim] *= blocks.shape[0]
+    return jnp.moveaxis(blocks, 0, dim).reshape(shape)
 
 
 def passed_along(value, axis, steps):
@@ -99,7 +111,14 @@
         arrived = passed_along(moved, "seg", -1)
         current = jnp.where(seg_index == seg_count - 2 - relay_step, arrived, current)
     precond = precondition(current, query_acts[0], basis_in[0], basis_out[0, 0], eigenvalues[0, 0])
-    exchanged = lax.all_to_all(train_grads, "blk", split_axis=2, concat_axis=1, tiled=True)
+    size, position = (lax.axis_size("blk"), lax.axis_index("blk"))
+    blocks = in_blocks(train_grads, 2, size)
+    outs = [blocks[position]]
+    for step in range(1, size):
+        sent = blocks[(position + step) % size]
+        outs.append(lax.ppermute(sent, "blk", [(i, (i + step) % size) for i in range(size)]))
+    blocks = jnp.stack(outs)[(position - jnp.arange(size)) % size]
+    exchanged = joined_along(blocks, 1)
     grad_rows = exchanged[0]
     scores_part, group_rows = block_scores(
         grad_rows, lax.all_gather(train_acts, "blk", axis=1, tiled=True)[0], precond, TB

time: 126 us -> 105 us (0.83)
  other arithmetic: 24.9 us -> 2.48 us
  starting transfers between devices: 9.43 us -> 14 us
  local copies, waits for them, and re-layouts: 19.1 us -> 17.5 us
  matrix products: 22.4 us -> 23.9 us
    unnamed x1 -> x0, other arithmetic: 23.4 us -> none
    ppermute x0 -> x7, starting transfers between devices: none -> 9.85 us  [body(): lax.ppermute(sent, 'blk', [(i, (i + step) % size) for i in range(size)])]
    unnamed x25 -> x26, local copies, waits for them, and re-layouts: 13.9 us -> 6.06 us
    another operation x0 -> x10, local copies, waits for them, and re-layouts: none -> 7.01 us
    all_to_all x1 -> x0, starting transfers between devices: 5.33 us -> none  [body(): lax.all_to_all(train_grads, 'blk', split_axis=2, concat_axis=1, tiled=True)]
    all_to_all x1 -> x0, local copies, waits for them, and re-layouts: 1.48 us -> none  [body(): lax.all_to_all(train_grads, 'blk', split_axis=2, concat_axis=1, tiled=True)]
    dot_general x1, matrix products: 3.21 us -> 4.56 us  [precondition(): jnp.einsum('cd,qdf->qcf', outer_basis, scaled_core, preferred_element_typ...]
  transfers between devices with their start and end apart: 5 -> 11, of which waited for: 2 -> 3; matrix products, arithmetic and copies ran while one was open for 40% -> 24% of each run, Pallas kernels for 0% -> 0%
where the time goes in v1:
time: 105 us
  matrix products  23.9 us (23%)
  blocking collectives  23 us (22%)
  local copies, waits for them, and re-layouts  17.5 us (17%)
  between operations  14.4 us (14%)
  starting transfers between devices  14 us (13%)
  waiting for transfers between devices  9.59 us (9%)
  other arithmetic  2.48 us (2%)
    unnamed x1, blocking collectives  12.1 us
    psum x1, blocking collectives, body(): mine = lax.psum(mine, 'seg')  10.8 us
    ppermute x7, starting transfers between devices, body(): lax.ppermute(sent, 'blk', [(i, (i + step) % size) for i in range(size)])  9.85 us
    ppermute x3, waiting for transfers between devices, passed_along(): lax.ppermute(value, axis, [(source, source + steps) for source in range(f...  9.56 us
    dot_general x2, matrix products, one_batch(): jnp.einsum('bde,qde->bq', outer_prod, precond, preferred_element_type=jnp...  7.62 us
    another operation x9, local copies, waits for them, and re-layouts  7 us
    unnamed x26, local copies, waits for them, and re-layouts  6.06 us
    dot_general x2, matrix products, one_batch(): jnp.einsum('btd,bte->bde', grad_block, act_block, preferred_element_type=...  4.97 us
  transfers between devices with their start and end apart: 11, of which 3 were waited for; matrix products, arithmetic and copies ran while one was open for 24% of the time, Pallas kernels for 0%

profile of v1, /device:TPU:0, one launch (start us, length us, event | category | flops | bytes accessed | tf_op | source)
XLA Modules:
  0.0 104.9 jit_solution(17464067136881828164)
XLA Ops:
  6.5 1.7 %copy.30 = bf16[1,128,4096]{1,2,0:T(8,128)(2,1)S(1)} copy(bf16[1,128,4096]{2,1,0:T(8,128)(2,1)} %param.13) | data formatting | bytes 2097152 | tf_op args[1]
  8.3 0.8 constant_dynamic-slice_fusion
  9.1 1.7 %copy.32 = bf16[1,128,1,512]{3,1,2,0:T(8,128)(2,1)} copy(bf16[1,128,1,512]{1,3,2,0:T(8,128)(2,1)} %get-tuple-element.69) | data formatting | bytes 262144 | tf_op jit(solution)/shard_map/dynamic-slice.1
  11.3 1.7 %copy.33 = bf16[1,128,1,512]{3,1,2,0:T(8,128)(2,1)} copy(bf16[1,128,1,512]{1,3,2,0:T(8,128)(2,1)} %get-tuple-element.68) | data formatting | bytes 262144 | tf_op jit(solution)/shard_map/dynamic-slice.2
  12.9 2.5 %collective-permute-start.1 = (bf16[1,128,512]{2,1,0:T(8,128)(2,1)}, bf16[1,128,512]{2,1,0:T(8,128)(2,1)}, u32[]{:S(2)}, u32[]{:S(2)}) collective-permute-start(bf16[1,128,512]{2,1,0:T(8,128)(2,1)} %bitcast.8), channel_id=1, source_target_pairs={{0,2},{1,3},{2,4},{3,5},{4,6},{5,7},{6,0},{7,1},{8,10},{9,11},{10,... | collective-permute-start | bytes 393224 | tf_op jit(solution)/shard_map/ppermute | solution.py:119
  15.4 1.7 %copy.34 = bf16[1,128,1,512]{3,1,2,0:T(8,128)(2,1)} copy(bf16[1,128,1,512]{1,3,2,0:T(8,128)(2,1)} %get-tuple-element.67) | data formatting | bytes 262144 | tf_op jit(solution)/shard_map/dynamic-slice.3
  17.1 2.4 %collective-permute-start.2 = (bf16[1,128,512]{2,1,0:T(8,128)(2,1)}, bf16[1,128,512]{2,1,0:T(8,128)(2,1)}, u32[]{:S(2)}, u32[]{:S(2)}) collective-permute-start(bf16[1,128,512]{2,1,0:T(8,128)(2,1)} %bitcast.10), channel_id=1, source_target_pairs={{0,3},{1,4},{2,5},{3,6},{4,7},{5,0},{6,1},{7,2},{8,11},{9,12},{10,... | collective-permute-start | bytes 393224 | tf_op jit(solution)/shard_map/ppermute | solution.py:119
  19.5 0.8 copy.35
  20.8 0.9 fusion.15
  21.7 1.4 %collective-permute-start.7 = (bf16[4,32,512]{2,1,0:T(8,128)(2,1)}, bf16[4,32,512]{2,1,0:T(8,128)(2,1)}, u32[]{:S(2)}, u32[]{:S(2)}) collective-permute-start(bf16[4,32,512]{2,1,0:T(8,128)(2,1)} %fusion.15), channel_id=1, source_target_pairs={{8,0},{16,8},{24,16},{9,1},{17,9},{25,17},{10,2},{18,10},{26,18},{... | collective-permute-start | bytes 393224 | tf_op jit(solution)/shard_map/ppermute | solution.py:27
  23.3 1.1 %add_bitcast_fusion = f32[512,512]{1,0:T(8,128)} fusion(bf16[1,1,512,512]{3,2,1,0:T(8,128)(2,1)S(1)} %copy-done.3), kind=kLoop, calls=%fused_computation.23 | loop fusion | flops 524288 | bytes 1572864 | tf_op jit(solution)/shard_map/add | solution.py:55
  24.4 2.0 %fusion.16 = bf16[4,32,512]{2,1,0:T(8,128)(2,1)} fusion(bf16[1,1,512,512]{3,2,1,0:T(8,128)(2,1)} %param.15, bf16[1,4,32,512]{3,2,1,0:T(8,128)(2,1)} %param.20), kind=kOutput, calls=%fused_computation.22 | convolution fusion | flops 67174400 | bytes 786432 | tf_op jit(solution)/shard_map/qtid,ide->qtie/dot_general | solution.py:50
  29.3 1.6 %collective-permute-start.5 = (bf16[1,128,512]{2,1,0:T(8,128)(2,1)S(1)}, bf16[1,128,512]{2,1,0:T(8,128)(2,1)S(1)}, u32[]{:S(2)}, u32[]{:S(2)}) collective-permute-start(bf16[1,128,512]{2,1,0:T(8,128)(2,1)S(1)} %bitcast.118), channel_id=1, source_target_pairs={{0,6},{1,7},{2,0},{3,1},{4,2},{5,3},{6,4},{7,5},{8,14},{9,15},{10,... | collective-permute-start | bytes 393224 | tf_op jit(solution)/shard_map/ppermute | solution.py:119
  30.8 0.9 bitcast_dynamic-update-slice_fusion.6
  31.7 2.4 %collective-permute-start.6 = (bf16[1,128,512]{2,1,0:T(8,128)(2,1)S(1)}, bf16[1,128,512]{2,1,0:T(8,128)(2,1)S(1)}, u32[]{:S(2)}, u32[]{:S(2)}) collective-permute-start(bf16[1,128,512]{2,1,0:T(8,128)(2,1)S(1)} %bitcast.117), channel_id=1, source_target_pairs={{0,7},{1,0},{2,1},{3,2},{4,3},{5,4},{6,5},{7,6},{8,15},{9,8},{10,9... | collective-permute-start | bytes 393224 | tf_op jit(solution)/shard_map/ppermute | solution.py:119
  34.1 0.9 bitcast_dynamic-update-slice_fusion.5
  35.1 1.3 %collective-permute-start.8 = (bf16[4,32,512]{2,1,0:T(8,128)(2,1)S(1)}, bf16[4,32,512]{2,1,0:T(8,128)(2,1)S(1)}, u32[]{:S(2)}, u32[]{:S(2)}) collective-permute-start(bf16[4,32,512]{2,1,0:T(8,128)(2,1)S(1)} %add_convert_fusion.1), channel_id=1, source_target_pairs={{8,0},{16,8},{24,16},{9,1},{17,9},{25,17},{10,2},{18,10},{26,18},{... | collective-permute-start | bytes 393224 | tf_op jit(solution)/shard_map/ppermute | solution.py:27
  36.4 0.9 bitcast_dynamic-update-slice_fusion.4
  37.3 0.9 bitcast_dynamic-update-slice_fusion.3
  38.3 4.1 %collective-permute-done.8 = bf16[4,32,512]{2,1,0:T(8,128)(2,1)S(1)} collective-permute-done((bf16[4,32,512]{2,1,0:T(8,128)(2,1)S(1)}, bf16[4,32,512]{2,1,0:T(8,128)(2,1)S(1)}, u32[]{:S(2)}, u32[]{:S(2)}) %collective-permute-start.8) | collective-permute-done | bytes 131104 | tf_op jit(solution)/shard_map/ppermute | solution.py:27
  42.6 1.5 %collective-permute-start.9 = (bf16[4,32,512]{2,1,0:T(8,128)(2,1)S(1)}, bf16[4,32,512]{2,1,0:T(8,128)(2,1)S(1)}, u32[]{:S(2)}, u32[]{:S(2)}) collective-permute-start(bf16[4,32,512]{2,1,0:T(8,128)(2,1)S(1)} %add_convert_fusion), channel_id=1, source_target_pairs={{8,0},{16,8},{24,16},{9,1},{17,9},{25,17},{10,2},{18,10},{26,18},{... | collective-permute-start | bytes 393224 | tf_op jit(solution)/shard_map/ppermute | solution.py:27
  44.8 5.2 %collective-permute-done.9 = bf16[4,32,512]{2,1,0:T(8,128)(2,1)S(1)} collective-permute-done((bf16[4,32,512]{2,1,0:T(8,128)(2,1)S(1)}, bf16[4,32,512]{2,1,0:T(8,128)(2,1)S(1)}, u32[]{:S(2)}, u32[]{:S(2)}) %collective-permute-start.9) | collective-permute-done | bytes 131104 | tf_op jit(solution)/shard_map/ppermute | solution.py:27
  50.3 4.6 %fusion.13 = bf16[4,512,512]{2,1,0:T(8,128)(2,1)} fusion(bf16[4,32,512]{2,1,0:T(8,128)(2,1)S(1)} %bitcast.120, bf16[4,32,512]{2,1,0:T(8,128)(2,1)} %fusion.16, f32[512,512]{1,0:T(8,128)} %add_bitcast_fusion, bf16[1,1,512,512]{3,2,1,0:T(8,128)(2,1)S(1)} %copy-done), kind=kOutput, calls=%fused_computation.14 | convolution fusion | flops 1142947840 | bytes 3932160 | tf_op jit(solution)/shard_map/cd,qdf->qcf/dot_general | solution.py:58
  54.8 2.9 %fusion.10 = bf16[4,512,512]{2,1,0:T(8,128)(2,1)S(1)} fusion(bf16[4,512,512]{2,1,0:T(8,128)(2,1)} %fusion.13, bf16[1,1,512,512]{3,2,1,0:T(8,128)(2,1)S(1)} %copy-done.6), kind=kOutput, calls=%fused_computation.13 | convolution fusion | flops 1074790400 | bytes 4718592 | tf_op jit(solution)/shard_map/qcie,ife->qcif/dot_general | solution.py:62
  57.7 3.0 %copy.41 = bf16[4,512,512]{2,0,1:T(4,128)(2,1)} copy(bf16[4,512,512]{2,1,0:T(8,128)(2,1)S(1)} %fusion.10) | data formatting | bytes 4194304 | tf_op jit(solution)/shard_map/while | solution.py:87
  60.7 12.7 %while.10 = (s32[]{:T(128)}, f32[2,8,4]{1,0,2:T(2,128)S(1)}, bf16[2,8,64,512]{3,2,1,0:T(8,128)(2,1)S(1)}, bf16[2,8,64,512]{3,2,1,0:T(8,128)(2,1)}, bf16[4,512,512]{2,0,1:T(4,128)(2,1)}, /*index=5*/s32[]{:T(128)}, s32[]{:T(128)}) while((s32[]{:T(128)}, f32[2,8,4]{1,0,2:T(2,128)S(1)}, bf16[2,8,64,512]{3,2,1,0:T(8,128)(2,1)S(1)}, ...), condition=%wide.region_1.2_spmd, body=%wide.region_0.1_spmd.sunk | while | flops 287309824 | bytes 19924460 | solution.py:87
  60.7 2.5 %convolution_convert_fusion.4 = bf16[8,512,512]{2,1,0:T(8,128)(2,1)S(1)} fusion(bf16[2,8,64,512]{3,2,1,0:T(8,128)(2,1)} %get-tuple-element.119, s32[]{:T(128)} %get-tuple-element.109, bf16[2,8,64,512]{3,2,1,0:T(8,128)(2,1)S(1)} %get-tuple-element.118), kind=kOutput, calls=%fused_computation.3.clone.1 | convolution fusion | flops 270532608 | bytes 5243904 | tf_op jit(solution)/shard_map/while/body/eval_jaxpr/btd,bte->bde/dot_general | solution.py:82
  63.2 3.8 %fusion.49 = f32[8,4,1]{0,1,2:T(4,128)S(1)} fusion(bf16[4,512,512]{2,0,1:T(4,128)(2,1)S(1)} %copy-done.2, bf16[8,512,512]{2,1,0:T(8,128)(2,1)S(1)} %convolution_convert_fusion.4), kind=kOutput, calls=%fused_computation.1.clone.1 | convolution fusion | flops 16777216 | bytes 6291584 | tf_op jit(solution)/shard_map/while/body/eval_jaxpr/bde,qde->bq/dot_general | solution.py:85
  67.1 2.5 %convolution_convert_fusion.4 = bf16[8,512,512]{2,1,0:T(8,128)(2,1)S(1)} fusion(bf16[2,8,64,512]{3,2,1,0:T(8,128)(2,1)} %get-tuple-element.119, s32[]{:T(128)} %get-tuple-element.109, bf16[2,8,64,512]{3,2,1,0:T(8,128)(2,1)S(1)} %get-tuple-element.118), kind=kOutput, calls=%fused_computation.3.clone.1 | convolution fusion | flops 270532608 | bytes 5243904 | tf_op jit(solution)/shard_map/while/body/eval_jaxpr/btd,bte->bde/dot_general | solution.py:82
  69.6 3.8 %fusion.49 = f32[8,4,1]{0,1,2:T(4,128)S(1)} fusion(bf16[4,512,512]{2,0,1:T(4,128)(2,1)S(1)} %copy-done.2, bf16[8,512,512]{2,1,0:T(8,128)(2,1)S(1)} %convolution_convert_fusion.4), kind=kOutput, calls=%fused_computation.1.clone.1 | convolution fusion | flops 16777216 | bytes 6291584 | tf_op jit(solution)/shard_map/while/body/eval_jaxpr/bde,qde->bq/dot_general | solution.py:85
  73.8 12.1 %all-reduce = f32[4,16]{0,1:T(8,128)S(1)} all-reduce(f32[4,16]{0,1:T(8,128)S(1)} %fusion.29), channel_id=2, replica_groups=mesh['seg'=4,'blk'=8] {'blk'}, use_global_device_ids=true, to_apply=%region_2.3.clone | all-reduce | flops 64 | bytes 512
  86.6 10.8 %psum.7 = f32[4,2]{0,1:T(2,128)S(1)} all-reduce(f32[4,2]{0,1:T(2,128)S(1)} %constant_dynamic-slice_fusion.8), channel_id=1, replica_groups=mesh['seg'=4,'blk'=8] {'seg'}, use_global_device_ids=true, to_apply=%region_3.4 | all-reduce | flops 8 | bytes 64 | tf_op jit(solution)/shard_map/psum | solution.py:130
  (61 shorter events, 6.2 us)
Async XLA Ops:
  6.5 43.5 %copy-start = (bf16[1,1,512,512]{3,2,1,0:T(8,128)(2,1)S(1)}, bf16[1,1,512,512]{3,2,1,0:T(8,128)(2,1)}, u32[]{:S(2)}) copy-start(bf16[1,1,512,512]{3,2,1,0:T(8,128)(2,1)} %param.16) | copy-start | bytes 1572868
  6.5 54.1 %all-gather.2.cloned.1.call-start = ((), (), s32[]{:S(2)}) async-start(), calls=%async_computation | async-start | bytes 1179648 | tf_op jit(solution)/shard_map/all_gather | solution.py:124
  8.2 12.5 %copy-start.1 = (bf16[1,1,512,512]{3,2,1,0:T(8,128)(2,1)S(1)}, bf16[1,1,512,512]{3,2,1,0:T(8,128)(2,1)}, u32[]{:S(2)}) copy-start(bf16[1,1,512,512]{3,2,1,0:T(8,128)(2,1)} %param.18) | copy-start | bytes 1572868
  8.2 12.5 %copy-start.4 = (bf16[1,4,32,512]{3,2,1,0:T(8,128)(2,1)S(1)}, bf16[1,4,32,512]{3,2,1,0:T(8,128)(2,1)}, u32[]{:S(2)}) copy-start(bf16[1,4,32,512]{3,2,1,0:T(8,128)(2,1)} %param.19) | copy-start | bytes 393220
  8.2 12.5 %copy-start.5 = (bf16[4,32,512]{2,1,0:T(8,128)(2,1)S(1)}, bf16[4,32,512]{2,1,0:T(8,128)(2,1)}, u32[]{:S(2)}) copy-start(bf16[4,32,512]{2,1,0:T(8,128)(2,1)} %param.21) | copy-start | bytes 393220
  8.3 15.0 %copy-start.3 = (bf16[1,1,512,512]{3,2,1,0:T(8,128)(2,1)S(1)}, bf16[1,1,512,512]{3,2,1,0:T(8,128)(2,1)}, u32[]{:S(2)}) copy-start(bf16[1,1,512,512]{3,2,1,0:T(8,128)(2,1)} %param.17) | copy-start | bytes 1572868
  10.8 18.5 %collective-permute-start = (bf16[1,128,512]{2,1,0:T(8,128)(2,1)}, bf16[1,128,512]{2,1,0:T(8,128)(2,1)}, u32[]{:S(2)}, u32[]{:S(2)}) collective-permute-start(bf16[1,128,512]{2,1,0:T(8,128)(2,1)} %bitcast.6), channel_id=1, source_target_pairs={{0,1},{1,2},{2,3},{3,4},{4,5},{5,6},{6,7},{7,0},{8,9},{9,10},{10,1... | collective-permute-start | bytes 393224 | tf_op jit(solution)/shard_map/ppermute | solution.py:119
  12.9 18.8 %collective-permute-start.1 = (bf16[1,128,512]{2,1,0:T(8,128)(2,1)}, bf16[1,128,512]{2,1,0:T(8,128)(2,1)}, u32[]{:S(2)}, u32[]{:S(2)}) collective-permute-start(bf16[1,128,512]{2,1,0:T(8,128)(2,1)} %bitcast.8), channel_id=1, source_target_pairs={{0,2},{1,3},{2,4},{3,5},{4,6},{5,7},{6,0},{7,1},{8,10},{9,11},{10,... | collective-permute-start | bytes 393224 | tf_op jit(solution)/shard_map/ppermute | solution.py:119
  17.1 18.0 %collective-permute-start.2 = (bf16[1,128,512]{2,1,0:T(8,128)(2,1)}, bf16[1,128,512]{2,1,0:T(8,128)(2,1)}, u32[]{:S(2)}, u32[]{:S(2)}) collective-permute-start(bf16[1,128,512]{2,1,0:T(8,128)(2,1)} %bitcast.10), channel_id=1, source_target_pairs={{0,3},{1,4},{2,5},{3,6},{4,7},{5,0},{6,1},{7,2},{8,11},{9,12},{10,... | collective-permute-start | bytes 393224 | tf_op jit(solution)/shard_map/ppermute | solution.py:119
  20.2 17.0 %collective-permute-start.3 = (bf16[1,128,512]{2,1,0:T(8,128)(2,1)}, bf16[1,128,512]{2,1,0:T(8,128)(2,1)}, u32[]{:S(2)}, u32[]{:S(2)}) collective-permute-start(bf16[1,128,512]{2,1,0:T(8,128)(2,1)} %bitcast.12), channel_id=1, source_target_pairs={{0,4},{1,5},{2,6},{3,7},{4,0},{5,1},{6,2},{7,3},{8,12},{9,13},{10,... | collective-permute-start | bytes 393224 | tf_op jit(solution)/shard_map/ppermute | solution.py:119
  21.7 5.1 %copy-start.7 = (s32[8]{0:T(128)S(1)}, s32[8]{0:T(128)}, u32[]{:S(2)}) copy-start(s32[8]{0:T(128)} %param.14) | copy-start | bytes 100
  21.7 5.8 %copy-start.8 = (u32[32]{0:T(128)S(1)}, u32[32]{0:T(128)}, u32[]{:S(2)}) copy-start(u32[32]{0:T(128)} %constant.108) | copy-start | bytes 388
  21.7 7.3 %collective-permute-start.7 = (bf16[4,32,512]{2,1,0:T(8,128)(2,1)}, bf16[4,32,512]{2,1,0:T(8,128)(2,1)}, u32[]{:S(2)}, u32[]{:S(2)}) collective-permute-start(bf16[4,32,512]{2,1,0:T(8,128)(2,1)} %fusion.15), channel_id=1, source_target_pairs={{8,0},{16,8},{24,16},{9,1},{17,9},{25,17},{10,2},{18,10},{26,18},{... | collective-permute-start | bytes 393224 | tf_op jit(solution)/shard_map/ppermute | solution.py:27
  29.0 9.2 %collective-permute-start.4 = (bf16[1,128,512]{2,1,0:T(8,128)(2,1)S(1)}, bf16[1,128,512]{2,1,0:T(8,128)(2,1)S(1)}, u32[]{:S(2)}, u32[]{:S(2)}) collective-permute-start(bf16[1,128,512]{2,1,0:T(8,128)(2,1)S(1)} %bitcast.119), channel_id=1, source_target_pairs={{0,5},{1,6},{2,7},{3,0},{4,1},{5,2},{6,3},{7,4},{8,13},{9,14},{10,... | collective-permute-start | bytes 393224 | tf_op jit(solution)/shard_map/ppermute | solution.py:119
  29.3 9.0 %collective-permute-start.5 = (bf16[1,128,512]{2,1,0:T(8,128)(2,1)S(1)}, bf16[1,128,512]{2,1,0:T(8,128)(2,1)S(1)}, u32[]{:S(2)}, u32[]{:S(2)}) collective-permute-start(bf16[1,128,512]{2,1,0:T(8,128)(2,1)S(1)} %bitcast.118), channel_id=1, source_target_pairs={{0,6},{1,7},{2,0},{3,1},{4,2},{5,3},{6,4},{7,5},{8,14},{9,15},{10,... | collective-permute-start | bytes 393224 | tf_op jit(solution)/shard_map/ppermute | solution.py:119
  31.7 12.4 %collective-permute-start.6 = (bf16[1,128,512]{2,1,0:T(8,128)(2,1)S(1)}, bf16[1,128,512]{2,1,0:T(8,128)(2,1)S(1)}, u32[]{:S(2)}, u32[]{:S(2)}) collective-permute-start(bf16[1,128,512]{2,1,0:T(8,128)(2,1)S(1)} %bitcast.117), channel_id=1, source_target_pairs={{0,7},{1,0},{2,1},{3,2},{4,3},{5,4},{6,5},{7,6},{8,15},{9,8},{10,9... | collective-permute-start | bytes 393224 | tf_op jit(solution)/shard_map/ppermute | solution.py:119
  35.1 7.3 %collective-permute-start.8 = (bf16[4,32,512]{2,1,0:T(8,128)(2,1)S(1)}, bf16[4,32,512]{2,1,0:T(8,128)(2,1)S(1)}, u32[]{:S(2)}, u32[]{:S(2)}) collective-permute-start(bf16[4,32,512]{2,1,0:T(8,128)(2,1)S(1)} %add_convert_fusion.1), channel_id=1, source_target_pairs={{8,0},{16,8},{24,16},{9,1},{17,9},{25,17},{10,2},{18,10},{26,18},{... | collective-permute-start | bytes 393224 | tf_op jit(solution)/shard_map/ppermute | solution.py:27
  42.6 7.3 %collective-permute-start.9 = (bf16[4,32,512]{2,1,0:T(8,128)(2,1)S(1)}, bf16[4,32,512]{2,1,0:T(8,128)(2,1)S(1)}, u32[]{:S(2)}, u32[]{:S(2)}) collective-permute-start(bf16[4,32,512]{2,1,0:T(8,128)(2,1)S(1)} %add_convert_fusion), channel_id=1, source_target_pairs={{8,0},{16,8},{24,16},{9,1},{17,9},{25,17},{10,2},{18,10},{26,18},{... | collective-permute-start | bytes 393224 | tf_op jit(solution)/shard_map/ppermute | solution.py:27
  50.2 4.6 %copy-start.6 = (bf16[1,1,512,512]{3,2,1,0:T(8,128)(2,1)S(1)}, bf16[1,1,512,512]{3,2,1,0:T(8,128)(2,1)}, u32[]{:S(2)}) copy-start(bf16[1,1,512,512]{3,2,1,0:T(8,128)(2,1)} %param.15) | copy-start | bytes 1572868
  60.7 2.5 %copy-start.2 = (bf16[4,512,512]{2,0,1:T(4,128)(2,1)S(1)}, bf16[4,512,512]{2,0,1:T(4,128)(2,1)}, u32[]{:S(2)}) copy-start(bf16[4,512,512]{2,0,1:T(4,128)(2,1)} %get-tuple-element.120) | copy-start | bytes 6291460 | tf_op jit(solution)/shard_map/while
  67.1 2.5 %copy-start.2 = (bf16[4,512,512]{2,0,1:T(4,128)(2,1)S(1)}, bf16[4,512,512]{2,0,1:T(4,128)(2,1)}, u32[]{:S(2)}) copy-start(bf16[4,512,512]{2,0,1:T(4,128)(2,1)} %get-tuple-element.120) | copy-start | bytes 6291460 | tf_op jit(solution)/shard_map/while
Sparse Core Ops, SparseCore 0:
  23.2 30.8 all-gather.1
